TPU v7x, 256 devices: a whole 4x4x8 slice. The times are simulated.
256 devices in a mesh: batch: 128 (over z, y_lo, x, core), crop: 2 (over y_hi).
Axes of the slice: x: 4, y: 4 (y_hi: 2, y_lo: 2; y = y_hi * 2 + y_lo), z: 8, core: 2. Of those that a mesh axis runs over, the one named last changes fastest.
Arguments:
- voxels: bfloat16 [2, 131072, 512], P('crop', 'batch'), may hold values from -6 to 6
- phrases: bfloat16 [2048, 512], P('batch'), may hold values from -6 to 6
- pair_ids: int32 [2048], P('batch'), may hold values from 0 to 511
- margin_index: int32 [2, 128, 512], P('crop', 'batch'), may hold values from 0 to 1023, as said below
Outputs:
- voxel_grad: float32 [2, 131072, 512], P('crop', 'batch')
- phrase_grad: float32 [2048, 512], P('batch')
Inputs may be any that keep to these rules, and one draw needn't show every extreme that they name: Each list margin_index[c, b] holds 512 distinct rows of that batch index's 1024 rows; entry k of crop 0 and entry k of crop 1 at the same b show the same place.
All inputs are finite; a program needn't handle non-finite values.
Results may differ from a plain program's by a relative error of at most 0.0013.
Values may be sent and summed in bfloat16 or wider, within the bound.
A program may use at most 64 MiB of HBM per device.

v0:
```python
import math

import jax
import jax.numpy as jnp
from jax import lax
from jax.sharding import PartitionSpec as P

VOX_VOL = 256


def partner_2(value, axis, distance):
    mask = 2**distance
    pairs = [(source, source ^ mask) for source in range(lax.axis_size(axis))]
    return lax.ppermute(value, axis, pairs)


def local(voxels, phrases, pair_ids, margin_index):
    own_vox = voxels[0]
    rows, width = own_vox.shape
    scale = 1.0 / math.sqrt(width)
    owner_ids = lax.all_gather(pair_ids, "batch", axis=0, tiled=True)
    position = lax.axis_index("batch")
    volume = (position * rows + jnp.arange(rows, dtype=jnp.int32)) // VOX_VOL

    def tile(block, block_ids):
        sign = jnp.where(volume[:, None] == block_ids[None, :], 1.0, -1.0).astype(jnp.float32)
        logit = jnp.dot(own_vox, block.T, preferred_element_type=jnp.float32) * scale - 1.0
        dlogit = (-sign * jax.nn.sigmoid(-sign * logit)).astype(jnp.bfloat16)
        match_part = jnp.dot(dlogit, block, preferred_element_type=jnp.float32) * scale
        phrase_part = (
            lax.dot_general(
                dlogit, own_vox, (((0,), (0,)), ((), ())), preferred_element_type=jnp.float32
            )
            * scale
        )
        return (match_part, phrase_part)

    gathered = lax.all_gather(phrases, "batch", axis=0, tiled=True)
    total = gathered.shape[0]
    block_rows = math.gcd(total, 1024)
    num_blocks = total // block_rows
    blocks = gathered.reshape(num_blocks, block_rows, width)
    id_blocks = owner_ids.reshape(num_blocks, block_rows)

    def one_block(match_total, pieces):
        match_part, phrase_part = tile(pieces[0], pieces[1])
        return (match_total + match_part, phrase_part)

    match_grad, phrase_terms = lax.scan(
        one_block, jnp.zeros((rows, width), jnp.float32), (blocks, id_blocks)
    )
    own_partial = lax.psum_scatter(
        phrase_terms.reshape(total, width), "batch", scatter_dimension=0, tiled=True
    )
    phrase_grad = lax.psum(own_partial, "crop")
    picked = margin_index[0, 0]
    chosen = own_vox[picked]
    partner = partner_2(chosen, "crop", 0)
    voxel_grad = match_grad.at[picked].add(chosen.astype(jnp.float32) - partner.astype(jnp.float32))
    return (voxel_grad[None], phrase_grad)


def solution(mesh):
    placed = (P("crop", "batch", None), P("batch", None), P("batch"), P("crop", "batch", None))
    return jax.shard_map(
        local,
        mesh=mesh,
        in_specs=placed,
        out_specs=(P("crop", "batch", None), P("batch", None)),
        check_vma=False,
    )
```

profile of v0, /device:TPU:0, one launch (start us, length us, event | category | flops | bytes accessed | tf_op | source)
XLA Modules:
  0.0 844.9 jit_solution(14683347854786272296)
XLA Ops:
  7.2 0.0 all-gather.2.cloned.1.call-start
  7.2 0.7 all-gather.2.cloned.1.call-update
  7.9 0.0 reduce-scatter.2.cloned.1.call-start
  8.0 1.3 dynamic-slice
  10.0 0.9 dynamic-update-slice
  10.8 25.8 %all-reduce = s32[2048]{0:T(1024)S(1)} all-reduce(s32[2048]{0:T(1024)S(1)} %dynamic-update-slice), channel_id=1, replica_groups=mesh['batch'=128,'crop'=2] {'batch'}, use_global_device_ids=true, to_apply=%add | all-reduce | flops 2048 | bytes 16384
  36.6 188.7 %all-gather.2.cloned.1.call-done = bf16[2048,512]{1,0:T(8,128)(2,1)} async-done(((bf16[16,512]{1,0:T(8,128)(2,1)}), bf16[2048,512]{1,0:T(8,128)(2,1)}) %all-gather.2.cloned.1.call-update) | async-done | bytes 2097168 | tf_op jit(solution)/shard_map/all_gather | solution.py:38
  225.3 24.8 %while.15 = (s32[]{:T(128)}, f32[1024,512]{1,0:T(8,128)}, f32[2,1024,512]{2,1,0:T(8,128)}, s32[2,1024]{1,0:T(2,128)S(1)}, bf16[2,1024,512]{2,1,0:T(8,128)(2,1)},...) while((s32[]{:T(128)}, f32[1024,512]{1,0:T(8,128)}, ...), condition=%wide.region_1.2_spmd.clone, body=%wide.region_0.1_spmd.clone.sunk | while | flops 3234873344 | bytes 37770436 | solution.py:49
  225.3 0.0 copy-start
  225.4 3.9 fusion.38
  229.3 0.0 copy-start.4
  229.3 1.3 copy-done.4
  230.6 0.0 copy-done
  230.6 0.0 copy-start.3
  230.6 2.6 bitcast_dynamic-update-slice_fusion.2
  233.2 0.0 copy-done.3
  233.2 4.2 select_add_fusion.2
  237.5 0.0 copy-start
  237.5 3.9 fusion.38
  241.4 0.0 copy-start.4
  241.4 1.3 copy-done.4
  242.7 0.0 copy-done
  242.7 0.0 copy-start.3
  242.7 2.6 bitcast_dynamic-update-slice_fusion.2
  245.3 0.0 copy-done.3
  245.3 4.8 select_add_fusion.2
  250.1 0.0 copy-start.2
  250.1 0.0 copy-start.1
  250.1 0.0 reduce-scatter.2.cloned.1.call-update
  250.1 0.7 copy-done.2
  250.8 0.5 copy-done.1
  251.3 2.0 gather_fusion
  253.3 3.1 collective-permute-start
  256.4 11.9 %collective-permute-done = bf16[512,512]{1,0:T(8,128)(2,1)S(1)} collective-permute-done((bf16[512,512]{1,0:T(8,128)(2,1)S(1)}, bf16[512,512]{1,0:T(8,128)(2,1)S(1)}, u32[]{:S(2)}, u32[]{:S(2)}) %collective-permute-start) | collective-permute-done | bytes 524320 | tf_op jit(solution)/shard_map/ppermute | solution.py:14
  268.3 6.5 scatter_custom_fusion
  274.8 551.3 %reduce-scatter.2.cloned.1.call-done = f32[16,512]{1,0:T(8,128)} async-done(((f32[2048,512]{1,0:T(8,128)}), f32[16,512]{1,0:T(8,128)}) %reduce-scatter.2.cloned.1.call-update) | async-done | bytes 32784 | tf_op jit(solution)/shard_map/reduce_scatter | solution.py:52
  826.1 12.0 %psum.7 = f32[16,512]{1,0:T(8,128)} all-reduce(f32[16,512]{1,0:T(8,128)} %reduce-scatter.2.cloned.1.call-done), channel_id=1, replica_groups=mesh['batch'=128,'crop'=2] {'crop'}, use_global_device_ids=true, to_apply=%region_4.5 | all-reduce | flops 8192 | bytes 65536 | tf_op jit(solution)/shard_map/psum | solution.py:55
  (10 shorter events, 0.1 us)
Async XLA Ops:
  7.2 218.2 %all-gather.2.cloned.1.call-start = ((), (), s32[]{:S(2)}) async-start(), calls=%async_computation.1 | async-start | bytes 2113536 | tf_op jit(solution)/shard_map/all_gather | solution.py:38
  7.9 818.2 %reduce-scatter.2.cloned.1.call-start = ((), (), s32[]{:S(2)}) async-start(), calls=%async_computation.2 | async-start | bytes 4227072 | tf_op jit(solution)/shard_map/reduce_scatter | solution.py:52
  225.3 5.3 copy-start
  229.3 1.3 copy-start.4
  230.6 2.6 copy-start.3
  237.5 5.3 copy-start
  241.4 1.3 copy-start.4
  242.7 2.6 copy-start.3
  250.1 0.7 copy-start.2
  250.1 1.2 copy-start.1
  253.3 15.0 %collective-permute-start = (bf16[512,512]{1,0:T(8,128)(2,1)S(1)}, bf16[512,512]{1,0:T(8,128)(2,1)S(1)}, u32[]{:S(2)}, u32[]{:S(2)}) collective-permute-start(bf16[512,512]{1,0:T(8,128)(2,1)S(1)} %gather_fusion), channel_id=1, source_target_pairs={{0,1},{1,0},{2,3},{3,2},{4,5},{5,4},{6,7},{7,6},{8,9},{9,8},{10,11... | collective-permute-start | bytes 1572872 | tf_op jit(solution)/shard_map/ppermute | solution.py:14
Sparse Core Ops, SparseCore 0:
  9.8 215.4 all-gather.1
  250.3 575.7 reduce-scatter.1
where the time goes:
time: 845 us
  waiting for transfers between devices  753 us (89%)
  blocking collectives  37.8 us (4%)
  matrix products  22 us (3%)
  between operations  14.7 us (2%)
    reduce_scatter x1, waiting for transfers between devices, local(): lax.psum_scatter(phrase_terms.reshape(total, width), 'batch', scatter_dim...  551 us
    all_gather x1, waiting for transfers between devices, local(): gathered = lax.all_gather(phrases, 'batch', axis=0, tiled=True)  189 us
    unnamed x1, blocking collectives  25.8 us
  transfers between devices with their start and end apart: 3, of which 3 were waited for; matrix products, arithmetic and copies ran while one was open for 1% of the time, Pallas kernels for 0%

commit v1 on v0

v1 whole, which is shorter than its diff:
```python
import math

import jax
import jax.numpy as jnp
from jax import lax
from jax.experimental import pallas as pl
from jax.experimental.pallas import tpu as pltpu
from jax.sharding import PartitionSpec as P

MESH = pl.DeviceIdType.MESH
F32, BF16 = jnp.float32, jnp.bfloat16
NT = (((1,), (1,)), ((), ()))
TN = (((0,), (0,)), ((), ()))
VOX_VOL = 256
NX, NY, NZ = 4, 4, 8
OFFS = (0, 1, -1, 2, -2, 3, -3, 4)
BACK = tuple(OFFS.index(-o if o != 4 else 4) for o in OFFS)
GROUPS = ((0, 1), (1, 1), (2, 2), (4, 2), (6, 2))
PLANE = tuple(
    sorted(
        ((dx, dy) for dx in range(NX) for dy in range(NY) if (dx, dy) != (0, 0)),
        key=lambda d: -(min(d[0], NX - d[0]) + min(d[1], NY - d[1])),
    )
)
MARGIN_CHUNKS = 8
NUM_SEMS = 192


def kernel(
    vox_in, phr_in, ids_in, mrg_in, vg_out, pg_out,
    vx, ph, idb, idr, dt, st, ch, part, sb, rb, zs, zr, fs, fr, ms, mr, mo, vg,
    send_sem, recv_sem, loc_sem,
):
    rows, width = vox_in.shape
    own = phr_in.shape[0]
    half = width // 2
    scale = 1.0 / math.sqrt(width)
    b, c = lax.axis_index("batch"), lax.axis_index("crop")
    k, x, ylo, z = b % 2, (b // 2) % 4, (b // 8) % 2, b // 16
    y = c * 2 + ylo
    g, go = ylo * 4 + x, (1 - ylo) * 4 + x

    def at(dx=0, dy=0, dz=0, dk=0):
        xx, yy, zz, kk = (x + dx) % NX, (y + dy) % NY, (z + dz + NZ) % NZ, (k + dk) % 2
        return (((zz * 2 + yy % 2) * 4 + xx) * 2 + kk, yy // 2)

    count = [0]
    started = []

    def send(src, dst, where):
        n = count[0]
        count[0] += 1
        copy = pltpu.make_async_remote_copy(
            src_ref=src, dst_ref=dst, send_sem=send_sem.at[n], recv_sem=recv_sem.at[n],
            device_id=where, device_id_type=MESH,
        )
        copy.start()
        started.append(copy)
        return copy

    barrier = pltpu.get_barrier_semaphore()
    partners = [dict(dk=1)]
    partners += [dict(dz=o) for o in OFFS[1:]]
    partners += [dict(dx=dx, dy=dy) for dx, dy in PLANE]
    for p in partners:
        pl.semaphore_signal(barrier, inc=1, device_id=at(**p), device_id_type=MESH)

    mine = pl.ds(pl.multiple_of(k * rows, rows), rows)
    theirs = pl.ds(pl.multiple_of((1 - k) * rows, rows), rows)
    load_vox = pltpu.make_async_copy(vox_in, vx.at[mine], loc_sem.at[0])
    load_vox.start()
    load_phr = pltpu.make_async_copy(phr_in, ph.at[0, g], loc_sem.at[1])
    load_phr.start()
    idr[...] = jnp.zeros_like(idr)
    idr[:, 0:own] = ids_in[...]
    st[...] = (lax.broadcasted_iota(jnp.int32, st.shape, 0) == mrg_in[...]).astype(F32).astype(BF16)
    load_vox.wait()
    ch[...] = lax.dot_general(st[...], vx[mine, :], TN, preferred_element_type=F32).astype(BF16)
    load_phr.wait()
    idb[g, 0] = idr[...]
    pl.semaphore_wait(barrier, len(partners))

    margin = []
    step = ch.shape[0] // MARGIN_CHUNKS

    def send_margin(n):
        for _ in range(n):
            i = len(margin)
            if i < MARGIN_CHUNKS:
                piece = pl.ds(i * step, step)
                margin.append(send(ch.at[piece], part.at[piece], at(dy=2)))

    def forward(n, start, which):
        return [
            send(ph.at[pl.ds(start, n), which], ph.at[pl.ds(start, n), which], at(dx=dx))
            for dx in (2, 1, 3)
        ]

    def across(n, start):
        lo, hi = pl.ds(0, half), pl.ds(half, half)
        s = pl.ds(start, n)
        return [
            send(ph.at[s, g, :, lo], ph.at[s, g, :, lo], at(dy=1)),
            send(ph.at[s, g, :, hi], ph.at[s, g, :, hi], at(dy=3)),
        ]

    zc = {}
    for p in (7, 5, 6, 3, 4, 1, 2):
        zc[p] = send(phr_in, ph.at[BACK[p], g], at(dz=OFFS[p]))
    same, cross, other = [], [], []
    cross.append(across(1, 0))
    same.append(forward(1, 0, g))
    swap_vox = send(vox_in, vx.at[mine], at(dk=1))
    idc = {p: send(idr, idb.at[g, BACK[p]], at(dz=OFFS[p])) for p in range(1, NZ)}
    send_margin(1)
    for i, (start, n) in enumerate(GROUPS):
        if i == 0:
            continue
        for q in range(start, start + n):
            zc[BACK[q]].wait_recv()
        cross.append(across(n, start))
        same.append(forward(n, start, g))
        send_margin(2)
        for copy in cross[i - 1]:
            copy.wait_recv()
        pstart, pn = GROUPS[i - 1]
        other.append(forward(pn, pstart, go))
    for p in range(1, NZ):
        idc[p].wait_recv()
    id_y = send(idb.at[g], idb.at[g], at(dy=1 + 2 * ylo))
    id_same = [send(idb.at[g], idb.at[g], at(dx=dx)) for dx in (2, 1, 3)]
    for copy in cross[-1]:
        copy.wait_recv()
    pstart, pn = GROUPS[-1]
    other.append(forward(pn, pstart, go))
    id_y.wait_recv()
    id_other = [send(idb.at[go], idb.at[go], at(dx=dx)) for dx in (2, 1, 3)]
    send_margin(MARGIN_CHUNKS)
    swap_vox.wait_recv()
    for copy in id_same + id_other:
        copy.wait_recv()

    chunk = 1024
    total = vx.shape[0]
    first_vol = (b // 2) * (total // VOX_VOL)
    lane = lax.broadcasted_iota(jnp.int32, (128, 128), 1)
    row16 = lax.broadcasted_iota(jnp.int32, (128, 128), 0) % own
    pick = lane == row16

    def logits(i):
        for q, (start, n) in enumerate(GROUPS):
            if start // 2 == i:
                for copy in same[q] + other[q]:
                    copy.wait_recv()
        block = ph[2 * i : 2 * i + 2].reshape(256, width)
        cols = []
        for j in range(2):
            ids = jnp.broadcast_to(idb[:, 2 * i + j], (8, own, 128)).reshape(128, 128)
            cols.append(jnp.sum(jnp.where(pick, ids, 0).astype(F32), axis=1, keepdims=True))
        ids = jnp.concatenate(cols, axis=0)
        for t in range(total // chunk):
            c0 = t * chunk
            acc = lax.dot_general(block, vx[c0 : c0 + chunk, :], NT, preferred_element_type=F32)
            logit = acc * scale - 1.0
            vol = first_vol + (c0 + lax.broadcasted_iota(jnp.int32, (1, chunk), 1)) // VOX_VOL
            match = ids == vol.astype(F32)
            r = 1.0 / (1.0 + jnp.exp(jnp.where(match, logit, -logit)))
            dt[i * 256 : (i + 1) * 256, c0 : c0 + chunk] = jnp.where(match, -r, r).astype(BF16)

    pieces = {}

    def terms(i):
        r = jnp.dot(dt[i * 256 : (i + 1) * 256, :], vx[...], preferred_element_type=F32).astype(BF16)
        for gg in range(8):
            for h in range(2):
                for j in range(2):
                    r0 = j * 128 + gg * own
                    sb[i, gg, h, j] = r[r0 : r0 + own, h * half : (h + 1) * half]

    def send_terms(i):
        copies = []
        for n, (dx, dy) in enumerate(PLANE):
            yy = (y + dy) % NY
            gg = (yy % 2) * 4 + (x + dx) % NX
            copies.append(send(sb.at[i, gg, yy // 2], rb.at[i, n], at(dx=dx, dy=dy)))
        pieces[i] = copies

    zsum = {}

    def collect(i):
        for copy in pieces[i]:
            copy.wait_recv()
        acc = sb[i, g, c].astype(F32)
        for n in range(len(PLANE)):
            acc = acc + rb[i, n].astype(F32)
        zs[2 * i : 2 * i + 2] = acc
        for p in (2 * i, 2 * i + 1):
            if p:
                zsum[p] = send(zs.at[p], zr.at[BACK[p]], at(dz=OFFS[p]))

    logits(0)
    logits(1)
    terms(1)
    logits(2)
    send_terms(1)
    terms(2)
    logits(3)
    send_terms(2)
    terms(3)
    terms(0)
    send_terms(3)
    send_terms(0)

    flat = ph[...].reshape(NZ * 128, width)
    mstep = 512
    swaps = []
    for t in range(rows // mstep):
        cols = pl.ds(pl.multiple_of((1 - k) * rows + t * mstep, mstep), mstep)
        piece = pl.ds(t * mstep, mstep)
        ms[piece, :] = lax.dot_general(dt[:, cols], flat, TN, preferred_element_type=F32)
    for t in range(rows // mstep):
        piece = pl.ds(t * mstep, mstep)
        swaps.append(send(ms.at[piece], mr.at[piece], at(dk=1)))
    collect(1)
    for t in range(rows // mstep):
        cols = pl.ds(pl.multiple_of(k * rows + t * mstep, mstep), mstep)
        piece = pl.ds(t * mstep, mstep)
        mo[piece, :] = lax.dot_general(dt[:, cols], flat, TN, preferred_element_type=F32)
    collect(2)
    for copy in margin:
        copy.wait_recv()
    for copy in swaps:
        copy.wait_recv()
    fstep = 256
    stores = []
    for t in range(rows // fstep):
        piece = pl.ds(t * fstep, fstep)
        sel = st[piece, :]
        held = jnp.sum(sel.astype(F32), axis=1, keepdims=True)
        lower = pl.ds(pl.multiple_of(k * rows + t * fstep, fstep), fstep)
        extra = vx[lower, :].astype(F32) * held - jnp.dot(sel, part[...], preferred_element_type=F32)
        vg[piece, :] = (mo[piece, :] + mr[piece, :]) * scale + extra
    for t in range(rows // fstep):
        piece = pl.ds(t * fstep, fstep)
        store = pltpu.make_async_copy(vg.at[piece], vg_out.at[piece], loc_sem.at[2 + t])
        store.start()
        stores.append(store)
    collect(3)
    collect(0)
    acc = zs[0]
    for p in (7, 6, 5, 4, 3, 2, 1):
        zsum[p].wait_recv()
        acc = acc + zr[BACK[p]]
    fs[...] = acc * scale
    last = send(fs, fr, at(dy=2))
    for store in stores:
        store.wait()
    last.wait_recv()
    a, d = fs[...], fr[...]
    pg_out[:, 0:half] = jnp.where(c == 0, a, d)
    pg_out[:, half:width] = jnp.where(c == 0, d, a)
    for copy in started:
        copy.wait_send()
    assert count[0] <= NUM_SEMS


def local(voxels, phrases, pair_ids, margin_index):
    rows, width = voxels.shape[1:]
    own = phrases.shape[0]
    ovl = margin_index.shape[-1]
    half = width // 2
    vmem = pl.BlockSpec(memory_space=pltpu.VMEM)
    hbm = pl.BlockSpec(memory_space=pl.ANY)
    voxel_grad, phrase_grad = pl.pallas_call(
        kernel,
        name="grounding",
        out_shape=(
            jax.ShapeDtypeStruct((rows, width), F32),
            jax.ShapeDtypeStruct((own, width), F32),
        ),
        in_specs=[hbm, hbm, vmem, vmem],
        out_specs=(hbm, vmem),
        scratch_shapes=[
            pltpu.VMEM((2 * rows, width), BF16),
            pltpu.VMEM((NZ, 8, own, width), BF16),
            pltpu.VMEM((8, NZ, 1, 128), jnp.int32),
            pltpu.VMEM((1, 128), jnp.int32),
            pltpu.VMEM((NZ * 8 * own, 2 * rows), BF16),
            pltpu.VMEM((rows, ovl), BF16),
            pltpu.VMEM((ovl, width), BF16),
            pltpu.VMEM((ovl, width), BF16),
            pltpu.VMEM((4, 8, 2, 2, own, half), BF16),
            pltpu.VMEM((4, 15, 2, own, half), BF16),
            pltpu.VMEM((NZ, own, half), F32),
            pltpu.VMEM((NZ, own, half), F32),
            pltpu.VMEM((own, half), F32),
            pltpu.VMEM((own, half), F32),
            pltpu.VMEM((rows, width), F32),
            pltpu.VMEM((rows, width), F32),
            pltpu.VMEM((rows, width), F32),
            pltpu.VMEM((rows, width), F32),
            pltpu.SemaphoreType.DMA((NUM_SEMS,)),
            pltpu.SemaphoreType.DMA((NUM_SEMS,)),
            pltpu.SemaphoreType.DMA((8,)),
        ],
        compiler_params=pltpu.CompilerParams(
            collective_id=0, has_side_effects=True, vmem_limit_bytes=56 * 2**20
        ),
    )(voxels[0], phrases, pair_ids[None], margin_index[0])
    return (voxel_grad[None], phrase_grad)


def solution(mesh):
    placed = (P("crop", "batch", None), P("batch", None), P("batch"), P("crop", "batch", None))
    return jax.shard_map(
        local,
        mesh=mesh,
        in_specs=placed,
        out_specs=(P("crop", "batch", None), P("batch", None)),
        check_vma=False,
    )
```

time: 845 us -> 63.7 us (0.08)
  the two profiles are of different devices: /device:TPU:0 before, /device:TPU:32 now
where the time goes in v1:
time: 63.7 us; the launch traced here: 63.6 us
  Pallas kernels  59.2 us (93%)
  local copies, waits for them, and re-layouts  3.7 us (6%)
  between operations  0.65 us (1%)
    pallas_call x1, Pallas kernels, local(): pl.pallas_call(kernel, name='grounding', out_shape=(jax.ShapeDtypeStruct(...  59.2 us
    unnamed x4, local copies, waits for them, and re-layouts  3.7 us

profile of v1, /device:TPU:32, one launch (start us, length us, event | category | flops | bytes accessed | tf_op | source)
XLA Modules:
  0.0 63.6 jit_solution(8299133852344726320)
XLA Ops:
  0.6 59.2 %grounding.1 = (f32[1024,512]{1,0:T(8,128)}, f32[16,512]{1,0:T(8,128)}) custom-call(bf16[1024,512]{1,0:T(8,128)(2,1)} %bitcast.5, bf16[16,512]{1,0:T(8,128)(2,1)} %phr_in.1, s32[1,16]{1,0:T(1,128)} %bitcast.7, s32[1,512]{1,0:T(1,128)} %bitcast.6), custom_call_target="tpu_custom_call" | custom-call | tf_op jit(solution)/shard_map/grounding/pallas_call | solution.py:274
  59.9 0.0 copy-start
  59.9 3.1 %copy.8 = f32[1,1024,512]{2,1,0:T(8,128)} copy(f32[1,1024,512]{2,1,0:T(8,128)} %bitcast.4) | data formatting | bytes 4194304
  62.9 0.0 copy-done
  62.9 0.6 copy.9
Async XLA Ops:
  59.9 3.1 %copy-start = (f32[16,512]{1,0:T(8,128)S(1)}, f32[16,512]{1,0:T(8,128)}, u32[]{:S(2)}) copy-start(f32[16,512]{1,0:T(8,128)} %get-tuple-element.9) | copy-start | bytes 98308

commit v2 on v1

--- a/solution.py
+++ b/solution.py
@@ -23,12 +23,14 @@
     )
 )
 MARGIN_CHUNKS = 8
+EARLY = 1
+LATER = 1
 NUM_SEMS = 192
 
 
 def kernel(
     vox_in, phr_in, ids_in, mrg_in, vg_out, pg_out,
-    vx, ph, idb, idr, dt, st, ch, part, sb, rb, zs, zr, fs, fr, ms, mr, mo, vg,
+    vx, ph, idb, idr, dt, st, ch, part, sb, rb, zs, zr, fs, fr, ms, mr, mo, vg, idv, mrv, pg, fn,
     send_sem, recv_sem, loc_sem,
 ):
     rows, width = vox_in.shape
@@ -62,6 +64,7 @@
     partners = [dict(dk=1)]
     partners += [dict(dz=o) for o in OFFS[1:]]
     partners += [dict(dx=dx, dy=dy) for dx, dy in PLANE]
+    partners += [dict(dy=2, dz=1), dict(dy=2, dz=-1)]
     for p in partners:
         pl.semaphore_signal(barrier, inc=1, device_id=at(**p), device_id_type=MESH)
 
@@ -71,9 +74,15 @@
     load_vox.start()
     load_phr = pltpu.make_async_copy(phr_in, ph.at[0, g], loc_sem.at[1])
     load_phr.start()
+    load_ids = pltpu.make_async_copy(ids_in, idv, loc_sem.at[6])
+    load_ids.start()
+    load_mrg = pltpu.make_async_copy(mrg_in, mrv, loc_sem.at[7])
+    load_mrg.start()
+    load_ids.wait()
     idr[...] = jnp.zeros_like(idr)
-    idr[:, 0:own] = ids_in[...]
-    st[...] = (lax.broadcasted_iota(jnp.int32, st.shape, 0) == mrg_in[...]).astype(F32).astype(BF16)
+    idr[:, 0:own] = idv[...]
+    load_mrg.wait()
+    st[...] = (lax.broadcasted_iota(jnp.int32, st.shape, 0) == mrv[...]).astype(F32).astype(BF16)
     load_vox.wait()
     ch[...] = lax.dot_general(st[...], vx[mine, :], TN, preferred_element_type=F32).astype(BF16)
     load_phr.wait()
@@ -105,40 +114,39 @@
         ]
 
     zc = {}
+    idc = {p: send(idr, idb.at[g, BACK[p]], at(dz=OFFS[p])) for p in range(1, NZ)}
     for p in (7, 5, 6, 3, 4, 1, 2):
         zc[p] = send(phr_in, ph.at[BACK[p], g], at(dz=OFFS[p]))
     same, cross, other = [], [], []
     cross.append(across(1, 0))
     same.append(forward(1, 0, g))
     swap_vox = send(vox_in, vx.at[mine], at(dk=1))
-    idc = {p: send(idr, idb.at[g, BACK[p]], at(dz=OFFS[p])) for p in range(1, NZ)}
-    send_margin(1)
-    for i, (start, n) in enumerate(GROUPS):
-        if i == 0:
-            continue
+    send_margin(EARLY)
+
+    def relay(i):
+        start, n = GROUPS[i]
         for q in range(start, start + n):
             zc[BACK[q]].wait_recv()
         cross.append(across(n, start))
         same.append(forward(n, start, g))
-        send_margin(2)
-        for copy in cross[i - 1]:
+
+    def relay_other(i):
+        start, n = GROUPS[i]
+        for copy in cross[i]:
             copy.wait_recv()
-        pstart, pn = GROUPS[i - 1]
-        other.append(forward(pn, pstart, go))
+        other.append(forward(n, start, go))
+
+    relay(1)
+    relay_other(0)
     for p in range(1, NZ):
         idc[p].wait_recv()
-    id_y = send(idb.at[g], idb.at[g], at(dy=1 + 2 * ylo))
-    id_same = [send(idb.at[g], idb.at[g], at(dx=dx)) for dx in (2, 1, 3)]
-    for copy in cross[-1]:
-        copy.wait_recv()
-    pstart, pn = GROUPS[-1]
-    other.append(forward(pn, pstart, go))
-    id_y.wait_recv()
-    id_other = [send(idb.at[go], idb.at[go], at(dx=dx)) for dx in (2, 1, 3)]
-    send_margin(MARGIN_CHUNKS)
-    swap_vox.wait_recv()
-    for copy in id_same + id_other:
-        copy.wait_recv()
+    beside = 1 + 2 * ylo
+    ids_seen = [send(idb.at[g], idb.at[g], at(dx=dx, dy=beside)) for dx in (2, 1, 3, 0)]
+    ids_seen += [send(idb.at[g], idb.at[g], at(dx=dx)) for dx in (2, 1, 3)]
+    for i in (2, 3, 4):
+        relay(i)
+        relay_other(i - 1)
+        send_margin(LATER)
 
     chunk = 1024
     total = vx.shape[0]
@@ -185,7 +193,7 @@
             copies.append(send(sb.at[i, gg, yy // 2], rb.at[i, n], at(dx=dx, dy=dy)))
         pieces[i] = copies
 
-    zsum = {}
+    zsum, near = {}, []
 
     def collect(i):
         for copy in pieces[i]:
@@ -197,8 +205,15 @@
         for p in (2 * i, 2 * i + 1):
             if p:
                 zsum[p] = send(zs.at[p], zr.at[BACK[p]], at(dz=OFFS[p]))
-
+            if p == 1:
+                near.append(send(zs.at[p], fn, at(dy=2, dz=1)))
+
+    swap_vox.wait_recv()
+    for copy in ids_seen:
+        copy.wait_recv()
     logits(0)
+    relay_other(4)
+    send_margin(MARGIN_CHUNKS)
     logits(1)
     terms(1)
     logits(2)
@@ -248,17 +263,22 @@
     collect(3)
     collect(0)
     acc = zs[0]
-    for p in (7, 6, 5, 4, 3, 2, 1):
+    for p in (7, 6, 5, 4, 3, 2):
         zsum[p].wait_recv()
         acc = acc + zr[BACK[p]]
-    fs[...] = acc * scale
+    fs[...] = acc
     last = send(fs, fr, at(dy=2))
+    zsum[1].wait_recv()
     for store in stores:
         store.wait()
     last.wait_recv()
-    a, d = fs[...], fr[...]
-    pg_out[:, 0:half] = jnp.where(c == 0, a, d)
-    pg_out[:, half:width] = jnp.where(c == 0, d, a)
+    near[0].wait_recv()
+    a, d = (fs[...] + zr[BACK[1]]) * scale, (fr[...] + fn[...]) * scale
+    pg[:, 0:half] = jnp.where(c == 0, a, d)
+    pg[:, half:width] = jnp.where(c == 0, d, a)
+    store = pltpu.make_async_copy(pg, pg_out, loc_sem.at[8])
+    store.start()
+    store.wait()
     for copy in started:
         copy.wait_send()
     assert count[0] <= NUM_SEMS
@@ -269,8 +289,9 @@
     own = phrases.shape[0]
     ovl = margin_index.shape[-1]
     half = width // 2
-    vmem = pl.BlockSpec(memory_space=pltpu.VMEM)
-    hbm = pl.BlockSpec(memory_space=pl.ANY)
+    hbm = pl.BlockSpec(memory_space=pltpu.HBM)
+    any_space = pl.BlockSpec(memory_space=pl.ANY)
+    inputs = (voxels[0], phrases, pair_ids[None], margin_index[0])
     voxel_grad, phrase_grad = pl.pallas_call(
         kernel,
         name="grounding",
@@ -278,8 +299,8 @@
             jax.ShapeDtypeStruct((rows, width), F32),
             jax.ShapeDtypeStruct((own, width), F32),
         ),
-        in_specs=[hbm, hbm, vmem, vmem],
-        out_specs=(hbm, vmem),
+        in_specs=[hbm, hbm, hbm, hbm],
+        out_specs=(any_space, any_space),
         scratch_shapes=[
             pltpu.VMEM((2 * rows, width), BF16),
             pltpu.VMEM((NZ, 8, own, width), BF16),
@@ -299,14 +320,18 @@
             pltpu.VMEM((rows, width), F32),
             pltpu.VMEM((rows, width), F32),
             pltpu.VMEM((rows, width), F32),
+            pltpu.VMEM((1, own), jnp.int32),
+            pltpu.VMEM((1, ovl), jnp.int32),
+            pltpu.VMEM((own, width), F32),
+            pltpu.VMEM((own, half), F32),
             pltpu.SemaphoreType.DMA((NUM_SEMS,)),
             pltpu.SemaphoreType.DMA((NUM_SEMS,)),
-            pltpu.SemaphoreType.DMA((8,)),
+            pltpu.SemaphoreType.DMA((16,)),
         ],
         compiler_params=pltpu.CompilerParams(
-            collective_id=0, has_side_effects=True, vmem_limit_bytes=56 * 2**20
+            collective_id=0, has_side_effects=True, vmem_limit_bytes=24 * 2**20
         ),
-    )(voxels[0], phrases, pair_ids[None], margin_index[0])
+    )(*(pltpu.with_memory_space_constraint(a, pltpu.HBM) for a in inputs))
     return (voxel_grad[None], phrase_grad)
 
 

time: 63.7 us -> 57 us (0.89)
  Pallas kernels: 59.2 us -> 54.3 us
  local copies, waits for them, and re-layouts: 3.7 us -> 1.94 us
    pallas_call x1, Pallas kernels: 59.2 us -> 54.3 us  [local(): pl.pallas_call(kernel, name='grounding', out_shape=(jax.ShapeDtypeStruct(...]
    unnamed x4 -> x2, local copies, waits for them, and re-layouts: 3.7 us -> 1.94 us
where the time goes in v2:
time: 57 us; the launch traced here: 56.9 us
  Pallas kernels  54.3 us (95%)
  local copies, waits for them, and re-layouts  1.94 us (3%)
  between operations  0.64 us (1%)
    pallas_call x1, Pallas kernels, local(): pl.pallas_call(kernel, name='grounding', out_shape=(jax.ShapeDtypeStruct(...  54.3 us
    unnamed x2, local copies, waits for them, and re-layouts  1.94 us

profile of v2, /device:TPU:32, one launch (start us, length us, event | category | flops | bytes accessed | tf_op | source)
XLA Modules:
  0.0 56.9 jit_solution(12143759670887036251)
XLA Ops:
  0.6 54.3 %grounding.1 = (f32[1024,512]{1,0:T(8,128)S(1)}, f32[16,512]{1,0:T(8,128)S(1)}) custom-call(bf16[1024,512]{1,0:T(8,128)(2,1)} %bitcast.5, bf16[16,512]{1,0:T(8,128)(2,1)} %phr_in.1, s32[1,16]{1,0:T(1,128)} %bitcast.7, s32[1,512]{1,0:T(1,128)} %bitcast.6), custom_call_target="tpu_custom_call" | custom-call | tf_op jit(solution)/shard_map/grounding/pallas_call | solution.py:295
  54.9 1.3 %copy.8 = f32[1,1024,512]{2,1,0:T(8,128)} copy(f32[1,1024,512]{2,1,0:T(8,128)S(1)} %bitcast.4) | data formatting | bytes 4194304
  56.3 0.6 %copy.9 = f32[16,512]{1,0:T(8,128)} copy(f32[16,512]{1,0:T(8,128)S(1)} %get-tuple-element.9) | data formatting | bytes 65536

commit v3 on v2

--- a/solution.py
+++ b/solution.py
@@ -13,24 +13,27 @@
 TN = (((0,), (0,)), ((), ()))
 VOX_VOL = 256
 NX, NY, NZ = 4, 4, 8
-OFFS = (0, 1, -1, 2, -2, 3, -3, 4)
+OFFS = (0, -2, 1, -1, 3, 4, 2, -3)
 BACK = tuple(OFFS.index(-o if o != 4 else 4) for o in OFFS)
-GROUPS = ((0, 1), (1, 1), (2, 2), (4, 2), (6, 2))
+GROUPS = ((0, 1), (1, 1), (4, 2), (6, 2))
+NEXT = (2, 3)
 PLANE = tuple(
     sorted(
         ((dx, dy) for dx in range(NX) for dy in range(NY) if (dx, dy) != (0, 0)),
         key=lambda d: -(min(d[0], NX - d[0]) + min(d[1], NY - d[1])),
     )
 )
-MARGIN_CHUNKS = 8
-EARLY = 1
-LATER = 1
+MARGIN_CHUNKS = 16
+DIRECT = 2
+EARLY = 8
+LATER = 8
+MIDDLE = 5
 NUM_SEMS = 192
 
 
 def kernel(
     vox_in, phr_in, ids_in, mrg_in, vg_out, pg_out,
-    vx, ph, idb, idr, dt, st, ch, part, sb, rb, zs, zr, fs, fr, ms, mr, mo, vg, idv, mrv, pg, fn,
+    vx, ph, idb, dt, st, ch, part, sb, rb, zs, zr, fs, fr, ms, mr, mo, vg, mrv, pg, fn, tb, ub,
     send_sem, recv_sem, loc_sem,
 ):
     rows, width = vox_in.shape
@@ -64,29 +67,19 @@
     partners = [dict(dk=1)]
     partners += [dict(dz=o) for o in OFFS[1:]]
     partners += [dict(dx=dx, dy=dy) for dx, dy in PLANE]
-    partners += [dict(dy=2, dz=1), dict(dy=2, dz=-1)]
+    partners += [dict(dy=2, dz=dz) for dz in (2, -2, 3, -3, 4)]
     for p in partners:
         pl.semaphore_signal(barrier, inc=1, device_id=at(**p), device_id_type=MESH)
 
     mine = pl.ds(pl.multiple_of(k * rows, rows), rows)
-    theirs = pl.ds(pl.multiple_of((1 - k) * rows, rows), rows)
     load_vox = pltpu.make_async_copy(vox_in, vx.at[mine], loc_sem.at[0])
     load_vox.start()
     load_phr = pltpu.make_async_copy(phr_in, ph.at[0, g], loc_sem.at[1])
     load_phr.start()
-    load_ids = pltpu.make_async_copy(ids_in, idv, loc_sem.at[6])
+    load_ids = pltpu.make_async_copy(ids_in, idb.at[g, 0], loc_sem.at[6])
     load_ids.start()
     load_mrg = pltpu.make_async_copy(mrg_in, mrv, loc_sem.at[7])
     load_mrg.start()
-    load_ids.wait()
-    idr[...] = jnp.zeros_like(idr)
-    idr[:, 0:own] = idv[...]
-    load_mrg.wait()
-    st[...] = (lax.broadcasted_iota(jnp.int32, st.shape, 0) == mrv[...]).astype(F32).astype(BF16)
-    load_vox.wait()
-    ch[...] = lax.dot_general(st[...], vx[mine, :], TN, preferred_element_type=F32).astype(BF16)
-    load_phr.wait()
-    idb[g, 0] = idr[...]
     pl.semaphore_wait(barrier, len(partners))
 
     margin = []
@@ -113,21 +106,38 @@
             send(ph.at[s, g, :, hi], ph.at[s, g, :, hi], at(dy=3)),
         ]
 
+    def direct(n, start):
+        lo, hi = pl.ds(0, half), pl.ds(half, half)
+        s = pl.ds(start, n)
+        copies = []
+        for dx in (2, 1, 3, 0):
+            copies.append(send(ph.at[s, g, :, lo], ph.at[s, g, :, lo], at(dx=dx, dy=1)))
+            copies.append(send(ph.at[s, g, :, hi], ph.at[s, g, :, hi], at(dx=dx, dy=3)))
+        return copies
+
     zc = {}
-    idc = {p: send(idr, idb.at[g, BACK[p]], at(dz=OFFS[p])) for p in range(1, NZ)}
-    for p in (7, 5, 6, 3, 4, 1, 2):
+    idc = {p: send(ids_in, idb.at[g, BACK[p]], at(dz=OFFS[p])) for p in range(1, NZ)}
+    for p in (5, 4, 7, 6, 1):
         zc[p] = send(phr_in, ph.at[BACK[p], g], at(dz=OFFS[p]))
-    same, cross, other = [], [], []
-    cross.append(across(1, 0))
+    same, other, cross = [], [], {}
+    load_phr.wait()
+    other.append(direct(1, 0))
     same.append(forward(1, 0, g))
     swap_vox = send(vox_in, vx.at[mine], at(dk=1))
-    send_margin(EARLY)
+    load_mrg.wait()
+    st[...] = (lax.broadcasted_iota(jnp.int32, st.shape, 0) == mrv[...]).astype(F32).astype(BF16)
+    load_vox.wait()
+    ch[...] = lax.dot_general(st[...], vx[mine, :], TN, preferred_element_type=F32).astype(BF16)
+    load_ids.wait()
 
     def relay(i):
         start, n = GROUPS[i]
         for q in range(start, start + n):
             zc[BACK[q]].wait_recv()
-        cross.append(across(n, start))
+        if i < DIRECT:
+            other.append(direct(n, start))
+        else:
+            cross[i] = across(n, start)
         same.append(forward(n, start, g))
 
     def relay_other(i):
@@ -136,34 +146,35 @@
             copy.wait_recv()
         other.append(forward(n, start, go))
 
+    send_margin(EARLY)
     relay(1)
-    relay_other(0)
     for p in range(1, NZ):
         idc[p].wait_recv()
     beside = 1 + 2 * ylo
     ids_seen = [send(idb.at[g], idb.at[g], at(dx=dx, dy=beside)) for dx in (2, 1, 3, 0)]
     ids_seen += [send(idb.at[g], idb.at[g], at(dx=dx)) for dx in (2, 1, 3)]
-    for i in (2, 3, 4):
-        relay(i)
-        relay_other(i - 1)
-        send_margin(LATER)
+    relay(2)
+    for copy in same[0] + other[0]:
+        copy.wait_recv()
+    slabs = [send(ph.at[0], ph.at[BACK[p]], at(dz=OFFS[p])) for p in NEXT]
+    relay(3)
+    send_margin(LATER)
+    relay_other(2)
 
     chunk = 1024
     total = vx.shape[0]
     first_vol = (b // 2) * (total // VOX_VOL)
-    lane = lax.broadcasted_iota(jnp.int32, (128, 128), 1)
-    row16 = lax.broadcasted_iota(jnp.int32, (128, 128), 0) % own
+    lane = lax.broadcasted_iota(jnp.int32, (128, own), 1)
+    row16 = lax.broadcasted_iota(jnp.int32, (128, own), 0) % own
     pick = lane == row16
 
     def logits(i):
-        for q, (start, n) in enumerate(GROUPS):
-            if start // 2 == i:
-                for copy in same[q] + other[q]:
-                    copy.wait_recv()
+        for copy in arrivals[i]:
+            copy.wait_recv()
         block = ph[2 * i : 2 * i + 2].reshape(256, width)
         cols = []
         for j in range(2):
-            ids = jnp.broadcast_to(idb[:, 2 * i + j], (8, own, 128)).reshape(128, 128)
+            ids = jnp.broadcast_to(idb[:, 2 * i + j], (8, own, own)).reshape(128, own)
             cols.append(jnp.sum(jnp.where(pick, ids, 0).astype(F32), axis=1, keepdims=True))
         ids = jnp.concatenate(cols, axis=0)
         for t in range(total // chunk):
@@ -178,12 +189,18 @@
     pieces = {}
 
     def terms(i):
-        r = jnp.dot(dt[i * 256 : (i + 1) * 256, :], vx[...], preferred_element_type=F32).astype(BF16)
+        r = jnp.dot(dt[i * 256 : (i + 1) * 256, :], vx[...], preferred_element_type=F32)
         for gg in range(8):
             for h in range(2):
                 for j in range(2):
                     r0 = j * 128 + gg * own
-                    sb[i, gg, h, j] = r[r0 : r0 + own, h * half : (h + 1) * half]
+                    tile = r[r0 : r0 + own, h * half : (h + 1) * half]
+                    if i == 0 and j == 0:
+                        tile = tile + ub[0, gg, h].astype(F32) + ub[1, gg, h].astype(F32)
+                    if i == 1:
+                        tb[j, gg, h] = tile.astype(BF16)
+                    else:
+                        sb[i, gg, h, j] = tile.astype(BF16)
 
     def send_terms(i):
         copies = []
@@ -193,7 +210,7 @@
             copies.append(send(sb.at[i, gg, yy // 2], rb.at[i, n], at(dx=dx, dy=dy)))
         pieces[i] = copies
 
-    zsum, near = {}, []
+    zsum, near = {}, {}
 
     def collect(i):
         for copy in pieces[i]:
@@ -205,25 +222,29 @@
         for p in (2 * i, 2 * i + 1):
             if p:
                 zsum[p] = send(zs.at[p], zr.at[BACK[p]], at(dz=OFFS[p]))
-            if p == 1:
-                near.append(send(zs.at[p], fn, at(dy=2, dz=1)))
+                near[p] = send(zs.at[p], fn.at[BACK[p]], at(dy=2, dz=OFFS[p]))
 
     swap_vox.wait_recv()
     for copy in ids_seen:
         copy.wait_recv()
+    send_margin(MIDDLE)
+    arrivals = {0: same[1] + other[1], 1: slabs, 2: same[2] + other[2], 3: list(same[3])}
     logits(0)
-    relay_other(4)
+    relay_other(3)
     send_margin(MARGIN_CHUNKS)
+    arrivals[3] += other[3]
     logits(1)
     terms(1)
+    slabs_back = [send(tb.at[j], ub.at[j], at(dz=OFFS[p])) for j, p in enumerate(NEXT)]
     logits(2)
-    send_terms(1)
     terms(2)
+    send_terms(2)
     logits(3)
-    send_terms(2)
     terms(3)
+    send_terms(3)
+    for copy in slabs_back:
+        copy.wait_recv()
     terms(0)
-    send_terms(3)
     send_terms(0)
 
     flat = ph[...].reshape(NZ * 128, width)
@@ -236,12 +257,15 @@
     for t in range(rows // mstep):
         piece = pl.ds(t * mstep, mstep)
         swaps.append(send(ms.at[piece], mr.at[piece], at(dk=1)))
-    collect(1)
+    collect(2)
     for t in range(rows // mstep):
         cols = pl.ds(pl.multiple_of(k * rows + t * mstep, mstep), mstep)
         piece = pl.ds(t * mstep, mstep)
         mo[piece, :] = lax.dot_general(dt[:, cols], flat, TN, preferred_element_type=F32)
-    collect(2)
+    collect(3)
+    collect(0)
+    fs[...] = zs[0]
+    last = send(fs, fr, at(dy=2))
     for copy in margin:
         copy.wait_recv()
     for copy in swaps:
@@ -260,25 +284,20 @@
         store = pltpu.make_async_copy(vg.at[piece], vg_out.at[piece], loc_sem.at[2 + t])
         store.start()
         stores.append(store)
-    collect(3)
-    collect(0)
-    acc = zs[0]
-    for p in (7, 6, 5, 4, 3, 2):
+    acc, rest = zs[0], jnp.zeros_like(zs[0])
+    for p in (5, 4, 7, 6, 1):
         zsum[p].wait_recv()
+        near[p].wait_recv()
         acc = acc + zr[BACK[p]]
-    fs[...] = acc
-    last = send(fs, fr, at(dy=2))
-    zsum[1].wait_recv()
-    for store in stores:
-        store.wait()
+        rest = rest + fn[BACK[p]]
     last.wait_recv()
-    near[0].wait_recv()
-    a, d = (fs[...] + zr[BACK[1]]) * scale, (fr[...] + fn[...]) * scale
+    a, d = acc * scale, (fr[...] + rest) * scale
     pg[:, 0:half] = jnp.where(c == 0, a, d)
     pg[:, half:width] = jnp.where(c == 0, d, a)
     store = pltpu.make_async_copy(pg, pg_out, loc_sem.at[8])
     store.start()
-    store.wait()
+    for copy in stores + [store]:
+        copy.wait()
     for copy in started:
         copy.wait_send()
     assert count[0] <= NUM_SEMS
@@ -304,8 +323,7 @@
         scratch_shapes=[
             pltpu.VMEM((2 * rows, width), BF16),
             pltpu.VMEM((NZ, 8, own, width), BF16),
-            pltpu.VMEM((8, NZ, 1, 128), jnp.int32),
-            pltpu.VMEM((1, 128), jnp.int32),
+            pltpu.VMEM((8, NZ, 1, own), jnp.int32),
             pltpu.VMEM((NZ * 8 * own, 2 * rows), BF16),
             pltpu.VMEM((rows, ovl), BF16),
             pltpu.VMEM((ovl, width), BF16),
@@ -320,10 +338,11 @@
             pltpu.VMEM((rows, width), F32),
             pltpu.VMEM((rows, width), F32),
             pltpu.VMEM((rows, width), F32),
-            pltpu.VMEM((1, own), jnp.int32),
             pltpu.VMEM((1, ovl), jnp.int32),
             pltpu.VMEM((own, width), F32),
-            pltpu.VMEM((own, half), F32),
+            pltpu.VMEM((NZ, own, half), F32),
+            pltpu.VMEM((2, 8, 2, own, half), BF16),
+            pltpu.VMEM((2, 8, 2, own, half), BF16),
             pltpu.SemaphoreType.DMA((NUM_SEMS,)),
             pltpu.SemaphoreType.DMA((NUM_SEMS,)),
             pltpu.SemaphoreType.DMA((16,)),

time: 57 us -> 49.2 us (0.86)
  Pallas kernels: 54.3 us -> 46.1 us
    pallas_call x1, Pallas kernels: 54.3 us -> 46.1 us  [local(): pl.pallas_call(kernel, name='grounding', out_shape=(jax.ShapeDtypeStruct(...]
where the time goes in v3:
time: 49.2 us; the launch traced here: 48.6 us
  Pallas kernels  46.1 us (94%)
  local copies, waits for them, and re-layouts  1.94 us (4%)
  between operations  0.64 us (1%)
    pallas_call x1, Pallas kernels, local(): pl.pallas_call(kernel, name='grounding', out_shape=(jax.ShapeDtypeStruct(...  46.1 us
    unnamed x2, local copies, waits for them, and re-layouts  1.94 us

profile of v3, /device:TPU:32, one launch (start us, length us, event | category | flops | bytes accessed | tf_op | source)
XLA Modules:
  0.0 48.6 jit_solution(14774642967676886724)
XLA Ops:
  0.6 46.1 %grounding.1 = (f32[1024,512]{1,0:T(8,128)S(1)}, f32[16,512]{1,0:T(8,128)S(1)}) custom-call(bf16[1024,512]{1,0:T(8,128)(2,1)} %bitcast.5, bf16[16,512]{1,0:T(8,128)(2,1)} %phr_in.1, s32[1,16]{1,0:T(1,128)} %bitcast.7, s32[1,512]{1,0:T(1,128)} %bitcast.6), custom_call_target="tpu_custom_call" | custom-call | tf_op jit(solution)/shard_map/grounding/pallas_call | solution.py:314
  46.7 1.3 %copy.8 = f32[1,1024,512]{2,1,0:T(8,128)} copy(f32[1,1024,512]{2,1,0:T(8,128)S(1)} %bitcast.4) | data formatting | bytes 4194304
  48.0 0.6 %copy.9 = f32[16,512]{1,0:T(8,128)} copy(f32[16,512]{1,0:T(8,128)S(1)} %get-tuple-element.9) | data formatting | bytes 65536

commit v4 on v3

--- a/solution.py
+++ b/solution.py
@@ -17,6 +17,7 @@
 BACK = tuple(OFFS.index(-o if o != 4 else 4) for o in OFFS)
 GROUPS = ((0, 1), (1, 1), (4, 2), (6, 2))
 NEXT = (2, 3)
+NEAR = (1, 6, 7)
 PLANE = tuple(
     sorted(
         ((dx, dy) for dx in range(NX) for dy in range(NY) if (dx, dy) != (0, 0)),
@@ -25,10 +26,19 @@
 )
 MARGIN_CHUNKS = 16
 DIRECT = 2
-EARLY = 8
-LATER = 8
-MIDDLE = 5
+EARLY = 7
+LATER = 9
 NUM_SEMS = 192
+
+
+def encode(v):
+    return (v * jnp.abs(v)).astype(BF16)
+
+
+def decode(w):
+    w = w.astype(F32)
+    root = jnp.sqrt(jnp.abs(w))
+    return jnp.where(w < 0, -root, root)
 
 
 def kernel(
@@ -67,7 +77,7 @@
     partners = [dict(dk=1)]
     partners += [dict(dz=o) for o in OFFS[1:]]
     partners += [dict(dx=dx, dy=dy) for dx, dy in PLANE]
-    partners += [dict(dy=2, dz=dz) for dz in (2, -2, 3, -3, 4)]
+    partners += [dict(dy=2, dz=dz) for dz in (2, -2, 3, -3)]
     for p in partners:
         pl.semaphore_signal(barrier, inc=1, device_id=at(**p), device_id_type=MESH)
 
@@ -117,7 +127,7 @@
 
     zc = {}
     idc = {p: send(ids_in, idb.at[g, BACK[p]], at(dz=OFFS[p])) for p in range(1, NZ)}
-    for p in (5, 4, 7, 6, 1):
+    for p in (1, 5, 4, 7, 6):
         zc[p] = send(phr_in, ph.at[BACK[p], g], at(dz=OFFS[p]))
     same, other, cross = [], [], {}
     load_phr.wait()
@@ -159,7 +169,6 @@
     slabs = [send(ph.at[0], ph.at[BACK[p]], at(dz=OFFS[p])) for p in NEXT]
     relay(3)
     send_margin(LATER)
-    relay_other(2)
 
     chunk = 1024
     total = vx.shape[0]
@@ -196,11 +205,11 @@
                     r0 = j * 128 + gg * own
                     tile = r[r0 : r0 + own, h * half : (h + 1) * half]
                     if i == 0 and j == 0:
-                        tile = tile + ub[0, gg, h].astype(F32) + ub[1, gg, h].astype(F32)
+                        tile = tile + decode(ub[0, gg, h]) + decode(ub[1, gg, h])
                     if i == 1:
-                        tb[j, gg, h] = tile.astype(BF16)
+                        tb[j, gg, h] = encode(tile)
                     else:
-                        sb[i, gg, h, j] = tile.astype(BF16)
+                        sb[i, gg, h, j] = encode(tile)
 
     def send_terms(i):
         copies = []
@@ -215,24 +224,24 @@
     def collect(i):
         for copy in pieces[i]:
             copy.wait_recv()
-        acc = sb[i, g, c].astype(F32)
+        acc = decode(sb[i, g, c])
         for n in range(len(PLANE)):
-            acc = acc + rb[i, n].astype(F32)
+            acc = acc + decode(rb[i, n])
         zs[2 * i : 2 * i + 2] = acc
         for p in (2 * i, 2 * i + 1):
             if p:
                 zsum[p] = send(zs.at[p], zr.at[BACK[p]], at(dz=OFFS[p]))
+            if p in NEAR:
                 near[p] = send(zs.at[p], fn.at[BACK[p]], at(dy=2, dz=OFFS[p]))
 
     swap_vox.wait_recv()
     for copy in ids_seen:
         copy.wait_recv()
-    send_margin(MIDDLE)
-    arrivals = {0: same[1] + other[1], 1: slabs, 2: same[2] + other[2], 3: list(same[3])}
+    arrivals = {0: same[1] + other[1], 1: slabs}
     logits(0)
+    relay_other(2)
     relay_other(3)
-    send_margin(MARGIN_CHUNKS)
-    arrivals[3] += other[3]
+    arrivals[2], arrivals[3] = same[2] + other[2], same[3] + other[3]
     logits(1)
     terms(1)
     slabs_back = [send(tb.at[j], ub.at[j], at(dz=OFFS[p])) for j, p in enumerate(NEXT)]
@@ -264,7 +273,11 @@
         mo[piece, :] = lax.dot_general(dt[:, cols], flat, TN, preferred_element_type=F32)
     collect(3)
     collect(0)
-    fs[...] = zs[0]
+    acc = zs[0]
+    for p in (5, 4):
+        zsum[p].wait_recv()
+        acc = acc + zr[BACK[p]]
+    fs[...] = acc
     last = send(fs, fr, at(dy=2))
     for copy in margin:
         copy.wait_recv()
@@ -284,8 +297,8 @@
         store = pltpu.make_async_copy(vg.at[piece], vg_out.at[piece], loc_sem.at[2 + t])
         store.start()
         stores.append(store)
-    acc, rest = zs[0], jnp.zeros_like(zs[0])
-    for p in (5, 4, 7, 6, 1):
+    rest = jnp.zeros_like(acc)
+    for p in (7, 6, 1):
         zsum[p].wait_recv()
         near[p].wait_recv()
         acc = acc + zr[BACK[p]]

time: 49.2 us -> 48.2 us (0.980)
  Pallas kernels: 46.1 us -> 44.9 us
    pallas_call x1, Pallas kernels: 46.1 us -> 44.9 us  [local(): pl.pallas_call(kernel, name='grounding', out_shape=(jax.ShapeDtypeStruct(...]
where the time goes in v4:
time: 48.2 us; the launch traced here: 47.5 us
  Pallas kernels  44.9 us (93%)
  local copies, waits for them, and re-layouts  1.94 us (4%)
  between operations  0.64 us (1%)
    pallas_call x1, Pallas kernels, local(): pl.pallas_call(kernel, name='grounding', out_shape=(jax.ShapeDtypeStruct(...  44.9 us
    unnamed x2, local copies, waits for them, and re-layouts  1.94 us

profile of v4, /device:TPU:32, one launch (start us, length us, event | category | flops | bytes accessed | tf_op | source)
XLA Modules:
  0.0 47.5 jit_solution(8133064219162438402)
XLA Ops:
  0.6 44.9 %grounding.1 = (f32[1024,512]{1,0:T(8,128)S(1)}, f32[16,512]{1,0:T(8,128)S(1)}) custom-call(bf16[1024,512]{1,0:T(8,128)(2,1)} %bitcast.5, bf16[16,512]{1,0:T(8,128)(2,1)} %phr_in.1, s32[1,16]{1,0:T(1,128)} %bitcast.7, s32[1,512]{1,0:T(1,128)} %bitcast.6), custom_call_target="tpu_custom_call" | custom-call | tf_op jit(solution)/shard_map/grounding/pallas_call | solution.py:327
  45.5 1.3 %copy.8 = f32[1,1024,512]{2,1,0:T(8,128)} copy(f32[1,1024,512]{2,1,0:T(8,128)S(1)} %bitcast.4) | data formatting | bytes 4194304
  46.9 0.6 %copy.9 = f32[16,512]{1,0:T(8,128)} copy(f32[16,512]{1,0:T(8,128)S(1)} %get-tuple-element.9) | data formatting | bytes 65536

commit v5 on v4

--- a/solution.py
+++ b/solution.py
@@ -26,8 +26,8 @@
 )
 MARGIN_CHUNKS = 16
 DIRECT = 2
-EARLY = 7
-LATER = 9
+EARLY = 6
+LATER = 10
 NUM_SEMS = 192
 
 

time: 48.2 us -> 50.5 us (1.048); the launches traced: 47.5 us -> 50.4 us
  Pallas kernels: 44.9 us -> 47.8 us
    pallas_call x1, Pallas kernels: 44.9 us -> 47.8 us  [local(): pl.pallas_call(kernel, name='grounding', out_shape=(jax.ShapeDtypeStruct(...]
where the time goes in v5:
time: 50.5 us; the launch traced here: 50.4 us
  Pallas kernels  47.8 us (95%)
  local copies, waits for them, and re-layouts  1.94 us (4%)
  between operations  0.64 us (1%)
    pallas_call x1, Pallas kernels, local(): pl.pallas_call(kernel, name='grounding', out_shape=(jax.ShapeDtypeStruct(...  47.8 us
    unnamed x2, local copies, waits for them, and re-layouts  1.94 us

profile of v5, /device:TPU:32, one launch (start us, length us, event | category | flops | bytes accessed | tf_op | source)
XLA Modules:
  0.0 50.4 jit_solution(1613123946552784823)
XLA Ops:
  0.6 47.8 %grounding.1 = (f32[1024,512]{1,0:T(8,128)S(1)}, f32[16,512]{1,0:T(8,128)S(1)}) custom-call(bf16[1024,512]{1,0:T(8,128)(2,1)} %bitcast.5, bf16[16,512]{1,0:T(8,128)(2,1)} %phr_in.1, s32[1,16]{1,0:T(1,128)} %bitcast.7, s32[1,512]{1,0:T(1,128)} %bitcast.6), custom_call_target="tpu_custom_call" | custom-call | tf_op jit(solution)/shard_map/grounding/pallas_call | solution.py:327
  48.4 1.3 %copy.8 = f32[1,1024,512]{2,1,0:T(8,128)} copy(f32[1,1024,512]{2,1,0:T(8,128)S(1)} %bitcast.4) | data formatting | bytes 4194304
  49.8 0.6 %copy.9 = f32[16,512]{1,0:T(8,128)} copy(f32[16,512]{1,0:T(8,128)S(1)} %get-tuple-element.9) | data formatting | bytes 65536
